TPU v7x, 32 devices: a whole 2x2x4 slice. The times are simulated.
32 devices in a mesh: grp: 2 (over y), row: 4 (over x, core), col: 4 (over z).
Axes of the slice: x: 2, y: 2, z: 4, core: 2. Of those that a mesh axis runs over, the one named last changes fastest.
Arguments:
- dosage: float32 [16384, 2048], P(('grp', 'row'), 'col'), parts along dimension 0, as said below
- phenotypes: float32 [16384, 64], P(('grp', 'row'), 'col'), parts along dimension 0, may hold values from -6 to 6
- solution: float32 [4096, 64], P(('grp', 'col')), parts along dimension 0, may hold values from -6 to 6
- inverse_factor: float32 [4096, 2048], P(('grp', 'col'), 'row'), parts along dimension 0, as said below
Outputs:
- residual: float32 [16384, 64], P(('grp', 'row'), 'col'), parts along dimension 0
- correction: float32 [4096, 64], P(('grp', 'col')), parts along dimension 0
There are 2 independent parts, one for each index of `grp`. A program takes and returns all parts, laid end to end along the dimension named above; each array names one. Nothing has to cross between parts.
Inputs may be any that keep to these rules, and one draw needn't show every extreme that they name: `dosage`: dense real-valued entries. `inverse_factor`: upper triangular: entries below the diagonal are zero, diagonal entries positive; a given preconditioner, not derived from the slab's values.
All inputs are finite; a program needn't handle non-finite values.
Results may differ from a plain program's by a relative error of at most 0.00013.
Values sent between devices are 32-bit elements; how exact they have to be, the bound alone decides.
A program may use at most 64 MiB of HBM per device.

v0:
```python
import jax
import jax.numpy as jnp
from jax import lax
from jax.sharding import PartitionSpec as P

ITERS = 2


def transposed_product(left, right):
    return lax.dot_general(
        left,
        right,
        (((0,), (0,)), ((), ())),
        precision=lax.Precision.HIGHEST,
        preferred_element_type=jnp.float32,
    )


def plain_product(left, right):
    return jnp.dot(left, right, precision=lax.Precision.HIGHEST, preferred_element_type=jnp.float32)


def local(dosage, phenotypes, solution, inverse_factor):

    def residual_parts(field):
        fitted = plain_product(dosage, field)
        own = phenotypes - lax.psum_scatter(fitted, "col", scatter_dimension=1, tiled=True)
        return (own, own)

    field = solution
    total = jnp.zeros_like(solution)
    for step in range(ITERS):
        own, whole = residual_parts(field)
        partial_value = transposed_product(dosage, lax.all_gather(own, "col", axis=1, tiled=True))
        inner = lax.psum(transposed_product(inverse_factor, lax.psum(partial_value, "row")), "col")
        change = lax.psum(plain_product(inverse_factor, inner), "row")
        field = field + change
        total = total + change
    own, whole = residual_parts(field)
    return (own, total)


def solution(mesh):
    return jax.shard_map(
        local,
        mesh=mesh,
        in_specs=(
            P(("grp", "row"), "col"),
            P(("grp", "row"), "col"),
            P(("grp", "col"), None),
            P(("grp", "col"), "row"),
        ),
        out_specs=(P(("grp", "row"), "col"), P(("grp", "col"), None)),
        check_vma=False,
    )
```

profile of v0, /device:TPU:0, one launch (start us, length us, event | category | flops | bytes accessed | tf_op | source)
XLA Modules:
  0.0 355.0 jit_solution(17227823966330348009)
XLA Ops:
  7.2 7.2 %fusion.1 = f32[2048,64]{0,1:T(8,128)} fusion(f32[2048,512]{1,0:T(8,128)} %param.4, f32[512,64]{0,1:T(8,128)} %param.6), kind=kOutput, calls=%fused_computation.9 | convolution fusion | flops 805306368 | bytes 4849664 | tf_op jit(solution)/shard_map/dot_general | solution.py:20
  14.5 0.0 all-reduce.7.cloned.1.call-start
  14.5 24.7 %reduce-scatter.4.cloned.1.call-done = f32[2048,16]{0,1:T(8,128)} async-done(((f32[2048,64]{0,1:T(8,128)}), f32[2048,16]{0,1:T(8,128)}) %reduce-scatter.4.cloned.1.call-update) | async-done | bytes 131088 | tf_op jit(solution)/shard_map/reduce_scatter | solution.py:27
  39.2 0.9 sub.9
  40.1 15.5 %all_gather.6 = f32[2048,64]{0,1:T(8,128)S(1)} all-gather(f32[2048,16]{0,1:T(8,128)S(1)} %sub.9), channel_id=1, replica_groups=mesh['grp'=2,'row'=4,'col'=4] {'col'}, dimensions={1}, use_global_device_ids=true | all-gather | bytes 655360 | tf_op jit(solution)/shard_map/all_gather | solution.py:34
  55.6 5.5 %convolution_bitcast_fusion.3 = f32[512,64]{0,1:T(8,128)} fusion(f32[2048,64]{0,1:T(8,128)S(1)} %all_gather.6, f32[2048,512]{1,0:T(8,128)} %param.4), kind=kOutput, calls=%fused_computation.3 | convolution fusion | flops 805306368 | bytes 4849664 | tf_op jit(solution)/shard_map/dot_general | solution.py:10
  61.1 0.0 all-reduce.9.cloned.1.call-start
  61.2 30.3 %all-reduce.7.cloned.1.call-done = f32[512,64]{0,1:T(8,128)} async-done(((f32[512,64]{0,1:T(8,128)}), f32[512,64]{0,1:T(8,128)}) %all-reduce.7.cloned.1.call-update) | async-done | bytes 131088 | tf_op jit(solution)/shard_map/psum | solution.py:35
  91.5 2.3 convolution_bitcast_fusion.7
  93.8 0.0 all-reduce.11.cloned.1.call-start
  93.9 35.2 %all-reduce.9.cloned.1.call-done = f32[512,64]{0,1:T(8,128)} async-done(((f32[512,64]{0,1:T(8,128)}), f32[512,64]{0,1:T(8,128)}) %all-reduce.9.cloned.1.call-update) | async-done | bytes 131088 | tf_op jit(solution)/shard_map/psum | solution.py:35
  129.1 2.7 convolution_bitcast_fusion.6
  131.8 0.0 reduce-scatter.6.cloned.1.call-start
  131.8 31.6 %all-reduce.11.cloned.1.call-done = f32[512,64]{0,1:T(8,128)} async-done(((f32[512,64]{0,1:T(8,128)}), f32[512,64]{0,1:T(8,128)}) %all-reduce.11.cloned.1.call-update) | async-done | bytes 131088 | tf_op jit(solution)/shard_map/psum | solution.py:36
  163.4 0.9 add.27
  164.3 7.0 %convolution_bitcast_fusion.1 = f32[2048,64]{0,1:T(8,128)} fusion(f32[512,64]{0,1:T(8,128)S(1)} %add.27, f32[2048,512]{1,0:T(8,128)} %param.4), kind=kOutput, calls=%fused_computation.1 | convolution fusion | flops 805306368 | bytes 4849664 | tf_op jit(solution)/shard_map/dot_general | solution.py:20
  171.4 21.9 %reduce-scatter.6.cloned.1.call-done = f32[2048,16]{0,1:T(8,128)} async-done(((f32[2048,64]{0,1:T(8,128)}), f32[2048,16]{0,1:T(8,128)}) %reduce-scatter.6.cloned.1.call-update) | async-done | bytes 131088 | tf_op jit(solution)/shard_map/reduce_scatter | solution.py:27
  193.4 0.9 sub.10
  194.3 15.6 %all_gather.7 = f32[2048,64]{0,1:T(8,128)S(1)} all-gather(f32[2048,16]{0,1:T(8,128)S(1)} %sub.10), channel_id=1, replica_groups=mesh['grp'=2,'row'=4,'col'=4] {'col'}, dimensions={1}, use_global_device_ids=true | all-gather | bytes 655360 | tf_op jit(solution)/shard_map/all_gather | solution.py:34
  209.9 5.5 %convolution_bitcast_fusion.2 = f32[512,64]{0,1:T(8,128)} fusion(f32[2048,64]{0,1:T(8,128)S(1)} %all_gather.7, f32[2048,512]{1,0:T(8,128)} %param.4), kind=kOutput, calls=%fused_computation.2 | convolution fusion | flops 805306368 | bytes 4849664 | tf_op jit(solution)/shard_map/dot_general | solution.py:10
  215.5 0.0 all-reduce.15.cloned.1.call-start
  215.5 30.2 %all-reduce.13.cloned.1.call-done = f32[512,64]{0,1:T(8,128)} async-done(((f32[512,64]{0,1:T(8,128)}), f32[512,64]{0,1:T(8,128)}) %all-reduce.13.cloned.1.call-update) | async-done | bytes 131088 | tf_op jit(solution)/shard_map/psum | solution.py:35
  245.7 2.3 convolution_bitcast_fusion.5
  248.1 0.0 all-reduce.17.cloned.1.call-start
  248.1 35.2 %all-reduce.15.cloned.1.call-done = f32[512,64]{0,1:T(8,128)} async-done(((f32[512,64]{0,1:T(8,128)}), f32[512,64]{0,1:T(8,128)}) %all-reduce.15.cloned.1.call-update) | async-done | bytes 131088 | tf_op jit(solution)/shard_map/psum | solution.py:35
  283.3 2.7 convolution_bitcast_fusion.4
  286.0 0.0 reduce-scatter.8.cloned.1.call-start
  286.1 31.6 %all-reduce.17.cloned.1.call-done = f32[512,64]{0,1:T(8,128)} async-done(((f32[512,64]{0,1:T(8,128)}), f32[512,64]{0,1:T(8,128)}) %all-reduce.17.cloned.1.call-update) | async-done | bytes 131088 | tf_op jit(solution)/shard_map/psum | solution.py:36
  317.7 7.1 %convolution_bitcast_fusion = f32[2048,64]{0,1:T(8,128)} fusion(f32[2048,512]{1,0:T(8,128)} %param.4, f32[512,64]{0,1:T(8,128)S(1)} %add.27, f32[512,64]{0,1:T(8,128)} %all-reduce.17.cloned.1.call-done), kind=kOutput, calls=%fused_computation | convolution fusion | flops 805339136 | bytes 4980736 | tf_op jit(solution)/shard_map/dot_general | solution.py:20
  324.9 0.7 add.29
  325.6 21.3 %reduce-scatter.8.cloned.1.call-done = f32[2048,16]{0,1:T(8,128)} async-done(((f32[2048,64]{0,1:T(8,128)}), f32[2048,16]{0,1:T(8,128)}) %reduce-scatter.8.cloned.1.call-update) | async-done | bytes 131088 | tf_op jit(solution)/shard_map/reduce_scatter | solution.py:27
  346.9 1.6 sub.11
  (21 shorter events, 0.3 us)
Async XLA Ops:
  7.2 84.3 %copy-start = (f32[512,512]{1,0:T(8,128)S(1)}, f32[512,512]{1,0:T(8,128)}, u32[]{:S(2)}) copy-start(f32[512,512]{1,0:T(8,128)} %param.7) | copy-start | bytes 3145732
  7.2 32.0 %copy-start.1 = (f32[2048,16]{0,1:T(8,128)S(1)}, f32[2048,16]{0,1:T(8,128)}, u32[]{:S(2)}) copy-start(f32[2048,16]{0,1:T(8,128)} %param.5) | copy-start | bytes 393220
  7.2 32.0 %reduce-scatter.4.cloned.1.call-start = ((), (), s32[]{:S(2)}) async-start(), calls=%async_computation.3 | async-start | bytes 655360 | tf_op jit(solution)/shard_map/reduce_scatter | solution.py:27
  14.5 77.0 %all-reduce.7.cloned.1.call-start = ((), (), s32[]{:S(2)}) async-start(), calls=%async_computation.4 | async-start | bytes 262144 | tf_op jit(solution)/shard_map/psum | solution.py:35
  40.1 123.3 %copy-start.2 = (f32[512,64]{0,1:T(8,128)S(1)}, f32[512,64]{0,1:T(8,128)}, u32[]{:S(2)}) copy-start(f32[512,64]{0,1:T(8,128)} %param.6) | copy-start | bytes 393220
  61.1 67.9 %all-reduce.9.cloned.1.call-start = ((), (), s32[]{:S(2)}) async-start(), calls=%async_computation.5 | async-start | bytes 262144 | tf_op jit(solution)/shard_map/psum | solution.py:35
  93.8 69.6 %all-reduce.11.cloned.1.call-start = ((), (), s32[]{:S(2)}) async-start(), calls=%async_computation.6 | async-start | bytes 262144 | tf_op jit(solution)/shard_map/psum | solution.py:36
  131.8 61.6 %reduce-scatter.6.cloned.1.call-start = ((), (), s32[]{:S(2)}) async-start(), calls=%async_computation.7 | async-start | bytes 655360 | tf_op jit(solution)/shard_map/reduce_scatter | solution.py:27
  171.4 74.3 %all-reduce.13.cloned.1.call-start = ((), (), s32[]{:S(2)}) async-start(), calls=%async_computation.8 | async-start | bytes 262144 | tf_op jit(solution)/shard_map/psum | solution.py:35
  215.5 109.4 %copy-start.3 = (f32[512,64]{0,1:T(8,128)S(1)}, f32[512,64]{0,1:T(8,128)}, u32[]{:S(2)}) copy-start(f32[512,64]{0,1:T(8,128)} %all-reduce.11.cloned.1.call-done) | copy-start | bytes 393220
  215.5 67.8 %all-reduce.15.cloned.1.call-start = ((), (), s32[]{:S(2)}) async-start(), calls=%async_computation.9 | async-start | bytes 262144 | tf_op jit(solution)/shard_map/psum | solution.py:35
  248.1 69.6 %all-reduce.17.cloned.1.call-start = ((), (), s32[]{:S(2)}) async-start(), calls=%async_computation.10 | async-start | bytes 262144 | tf_op jit(solution)/shard_map/psum | solution.py:36
  286.0 60.8 %reduce-scatter.8.cloned.1.call-start = ((), (), s32[]{:S(2)}) async-start(), calls=%async_computation.11 | async-start | bytes 655360 | tf_op jit(solution)/shard_map/reduce_scatter | solution.py:27
  317.7 7.2 %copy-start.4 = (f32[512,64]{0,1:T(8,128)S(1)}, f32[512,64]{0,1:T(8,128)}, u32[]{:S(2)}) copy-start(f32[512,64]{0,1:T(8,128)} %all-reduce.17.cloned.1.call-done) | copy-start | bytes 393220
Sparse Core Ops, SparseCore 0:
  14.6 24.5 reduce-scatter.3
  61.3 30.1 all-reduce.6
  94.4 34.6 all-reduce.8
  131.9 31.4 all-reduce.10
  171.5 21.8 reduce-scatter.5
  215.6 30.1 all-reduce.12
  248.6 34.6 all-reduce.14
  286.2 31.4 all-reduce.16
  325.0 21.8 reduce-scatter.7
where the time goes:
time: 355 us
  waiting for transfers between devices  262 us (74%)
  matrix products  42.4 us (12%)
  blocking collectives  31.1 us (9%)
  between operations  13.9 us (4%)
  other arithmetic  5.01 us (1%)
    psum x2, waiting for transfers between devices, local(): lax.psum(transposed_product(inverse_factor, lax.psum(partial_value, 'row'...  70.4 us
    reduce_scatter x3, waiting for transfers between devices, residual_parts(): lax.psum_scatter(fitted, 'col', scatter_dimension=1, tiled=True)  67.9 us
    psum x2, waiting for transfers between devices, local(): change = lax.psum(plain_product(inverse_factor, inner), 'row')  63.2 us
    psum x2, waiting for transfers between devices, local(): lax.psum(partial_value, 'row')  60.5 us
    all_gather x2, blocking collectives, local(): lax.all_gather(own, 'col', axis=1, tiled=True)  31.1 us
    dot_general x5, matrix products, plain_product(): jnp.dot(left, right, precision=lax.Precision.HIGHEST, preferred_element_t...  26.7 us
    dot_general x4, matrix products, transposed_product(): lax.dot_general(left, right, (((0,), (0,)), ((), ())), precision=lax.Prec...  15.6 us
  transfers between devices with their start and end apart: 9, of which 9 were waited for; matrix products, arithmetic and copies ran while one was open for 0% of the time, Pallas kernels for 0%

commit v1 on v0

v1 whole, which is shorter than its diff:
```python
import functools

import jax
import jax.numpy as jnp
from jax import lax
from jax.experimental import pallas as pl
from jax.experimental.pallas import tpu as pltpu
from jax.sharding import PartitionSpec as P

ITERS = 2
MESH = pl.DeviceIdType.MESH
F32 = jnp.float32
BF16 = jnp.bfloat16
NN = (((1,), (0,)), ((), ()))
NT = (((1,), (1,)), ((), ()))


def split(value):
    high = value.astype(BF16)
    low = (value - high.astype(F32)).astype(BF16)
    return high, low


def product(left, right_high, right_low, dims):
    count = left.shape[0] // 2
    main = lax.dot_general(left, right_high, dims, preferred_element_type=F32)
    rest = lax.dot_general(left[:count], right_low, dims, preferred_element_type=F32)
    return main[:count] + (main[count:] + rest)


def stacked(value):
    return jnp.concatenate(split(value), axis=0)


def kernel(cfg, dosage, pheno, start, factor, residual, correction, *scratch):
    (n_row, n_col, chunks, n_in) = cfg
    (d_f32, d_hi, d_lo, y_in, y_pad, f_in, field, r_f32, r_hi, r_lo,
     own, got_p, got_s, put_p, put_s,
     f_own, f_got_p, f_got_s, f_put_p, f_put_s,
     acc, pair_got, cross_put, cross_got, back_put, back_got,
     i_own, i_got_p, i_got_s, i_put_p, i_put_s, inner,
     load_sem, d_sem, a_sem, f_sem, pair_sem, cross_ssem, cross_rsem, i_sem) = scratch
    rows_c = d_hi.shape[1]
    n_p = field.shape[0]
    half = n_p // 2
    blk = pheno.shape[0]
    n_half = f_own.shape[1]
    width = f_own.shape[3]
    n_x = n_row // 2

    row = lax.axis_index("row")
    col = lax.axis_index("col")
    core = lax.rem(row, 2)
    x = row // 2
    partner = {"row": row + 1 - 2 * core}
    is_first = col == 0
    is_last = col == n_col - 1

    loads = []
    for k, (src, dst) in enumerate(((start, f_in), (pheno, y_in), (factor, r_f32))):
        loads.append(pltpu.make_async_copy(src, dst, load_sem.at[k]))

    def d_copy(c):
        return pltpu.make_async_copy(
            dosage.at[pl.ds(pl.multiple_of(c * rows_c, rows_c), rows_c), :], d_f32.at[c], d_sem.at[c])

    loads[0].start()
    loads[1].start()
    for c in range(chunks):
        d_copy(c).start()
    loads[2].start()

    barrier = pltpu.get_barrier_semaphore()

    @pl.when(col > 0)
    def _():
        pl.semaphore_signal(barrier, inc=1, device_id={"col": col - 1}, device_id_type=MESH)

    @pl.when(col < n_col - 1)
    def _():
        pl.semaphore_signal(barrier, inc=1, device_id={"col": col + 1}, device_id_type=MESH)

    pl.semaphore_signal(barrier, inc=1, device_id=partner, device_id_type=MESH)
    for d in range(1, n_x):
        other = lax.rem(x + d, n_x) * 2 + core
        pl.semaphore_signal(barrier, inc=1, device_id={"row": other}, device_id_type=MESH)

    loads[0].wait()
    loads[1].wait()
    field[...] = f_in[...]
    for c in range(chunks):
        y_c = y_in[:, c * rows_c:(c + 1) * rows_c]
        for b in range(n_col):
            y_pad[c, b * blk:(b + 1) * blk, :] = jnp.where(col == b, y_c, 0.0)

    up_down = jnp.where(is_first, 0, 1) + jnp.where(is_last, 0, 1)
    pl.semaphore_wait(barrier, n_x + up_down)

    def line(src, dst, sems, way, c, step):
        return pltpu.make_async_remote_copy(
            src_ref=src, dst_ref=dst, send_sem=sems.at[way, 0, c], recv_sem=sems.at[way, 1, c],
            device_id={"col": jnp.clip(col + step, 0, n_col - 1)}, device_id_type=MESH)

    def fit(c, f_cat):
        return product(f_cat, d_hi[c], d_lo[c], NT) - y_pad[c]

    def up(it, c, src):
        return line(src, got_p.at[it, c], a_sem.at[it], 0, c, 1)

    def down(it, c, src):
        return line(src, got_s.at[it, c], a_sem.at[it], 1, c, -1)

    def fit_and_sum(it):
        f_cat = stacked(field[...])

        def make(c, carry):
            if it == 0:
                d_copy(c).wait()
                high, low = split(d_f32[c])
                d_hi[c] = high
                d_lo[c] = low
            own[it, c] = fit(c, f_cat)

            @pl.when(is_first)
            def _():
                up(it, c, own.at[it, c]).start()

            @pl.when(is_last)
            def _():
                down(it, c, own.at[it, c]).start()
            return carry

        lax.fori_loop(0, chunks, make, 0)
        acc[...] = jnp.zeros_like(acc)
        middle = jnp.logical_and(col > 0, col < n_col - 1)
        lag = jnp.where(middle, 2 * (n_col - 1 - 2 * col), 0)
        lag_s = jnp.clip(lag, 0, chunks)
        lag_p = jnp.clip(-lag, 0, chunks)
        lag_max = min(chunks, 2 * max(n_col - 3, 0))

        def step(i, carry):
            c_p = i - lag_p
            c_s = i - lag_s

            @pl.when(jnp.logical_and(jnp.logical_and(c_p >= 0, c_p < chunks), col > 0))
            def _():
                up(it, c_p, own.at[it, c_p]).wait_recv()

                @pl.when(col < n_col - 1)
                def _():
                    put_p[it, c_p] = got_p[it, c_p] + own[it, c_p]
                    up(it, c_p, put_p.at[it, c_p]).start()

            @pl.when(jnp.logical_and(jnp.logical_and(c_s >= 0, c_s < chunks), col < n_col - 1))
            def _():
                down(it, c_s, own.at[it, c_s]).wait_recv()

                @pl.when(col > 0)
                def _():
                    put_s[it, c_s] = got_s[it, c_s] + own[it, c_s]
                    down(it, c_s, put_s.at[it, c_s]).start()

            c = i - lag_p - lag_s

            @pl.when(jnp.logical_and(c >= 0, c < chunks))
            def _():
                before = jnp.where(is_first, 0.0, got_p[it, c])
                after = jnp.where(is_last, 0.0, got_s[it, c])
                resid = before + own[it, c] + after
                acc[...] += product(stacked(resid), d_hi[c], d_lo[c], NN)
            return carry

        lax.fori_loop(0, chunks + lag_max, step, 0)

    def drain_sum(it):
        def step(c, carry):
            @pl.when(col < n_col - 1)
            def _():
                up(it, c, own.at[it, c]).wait_send()

            @pl.when(col > 0)
            def _():
                down(it, c, own.at[it, c]).wait_send()
            return carry

        lax.fori_loop(0, chunks, step, 0)

    def row_sum(k):
        for h in range(2):
            back_put[k, h] = acc[h * half:(h + 1) * half, :]
        first = pltpu.make_async_remote_copy(
            src_ref=back_put.at[k, 1 - core], dst_ref=pair_got.at[k],
            send_sem=pair_sem.at[k, 0], recv_sem=pair_sem.at[k, 1],
            device_id=partner, device_id_type=MESH)
        first.start()
        first.wait_recv()
        cross_put[k] = back_put[k, core] + pair_got[k]
        sends = []
        for d in range(1, n_x):
            other = lax.rem(x + d, n_x) * 2 + core
            sends.append(pltpu.make_async_remote_copy(
                src_ref=cross_put.at[k], dst_ref=cross_got.at[k, d - 1],
                send_sem=cross_ssem.at[k, d - 1], recv_sem=cross_rsem.at[k, d - 1],
                device_id={"row": other}, device_id_type=MESH))
            sends[-1].start()
        parts = [cross_put[k]]
        for d in range(1, n_x):
            sends[d - 1].wait_recv()
            parts.append(cross_got[k, d - 1])
        total = None
        for chip in range(n_x):
            here = parts[0]
            for d in range(1, n_x):
                here = jnp.where(lax.rem(x - d + n_x, n_x) == chip, parts[d], here)
            total = here if total is None else total + here
        back_got[k, 2] = total
        last = pltpu.make_async_remote_copy(
            src_ref=back_got.at[k, 2], dst_ref=back_got.at[k, core],
            send_sem=pair_sem.at[k, 2], recv_sem=pair_sem.at[k, 3],
            device_id=partner, device_id_type=MESH)
        last.start()
        last.wait_recv()
        theirs = back_got[k, 1 - core]
        mine = total
        low = jnp.where(core == 0, mine, theirs)
        high = jnp.where(core == 0, theirs, mine)
        acc[0:half, :] = low
        acc[half:, :] = high
        for copy in (first, last, *sends):
            copy.wait_send()

    n_rb = r_hi.shape[1]
    n_cb = r_hi.shape[0]
    active_last = ((row + 1) * n_rb + n_cb - 1) // n_cb - 1
    active_last = jnp.minimum(active_last, n_col - 1)
    wide_i = n_p // n_in

    def i_up(it, c, src):
        return line(src, i_got_p.at[it, c], i_sem.at[it], 0, c, 1)

    def i_down(it, c, src):
        return line(src, i_got_s.at[it, c], i_sem.at[it], 1, c, -1)

    def solve(it):
        if it == 0:
            loads[2].wait()
            high, low = split(r_f32[...])
            r_hi[...] = high
            r_lo[...] = low

        @pl.when(col <= active_last)
        def _():
            part = product(stacked(acc[...]), r_hi[...], r_lo[...], NN)
            for c in range(n_in):
                i_own[it, c] = part[c * wide_i:(c + 1) * wide_i]

            @pl.when(jnp.logical_and(is_first, active_last > 0))
            def _():
                for c in range(n_in):
                    i_up(it, c, i_own.at[it, c]).start()

            @pl.when(jnp.logical_and(col == active_last, active_last > 0))
            def _():
                for c in range(n_in):
                    i_down(it, c, i_own.at[it, c]).start()

            lag = jnp.where(jnp.logical_and(col > 0, col < active_last), 2 * (active_last - 2 * col), 0)
            lag_s = jnp.clip(lag, 0, n_in)
            lag_p = jnp.clip(-lag, 0, n_in)
            lag_max = min(n_in, 2 * max(n_col - 3, 0))

            def step(i, carry):
                c_p = i - lag_p
                c_s = i - lag_s

                @pl.when(jnp.logical_and(jnp.logical_and(c_p >= 0, c_p < n_in), col > 0))
                def _():
                    i_up(it, c_p, i_own.at[it, c_p]).wait_recv()

                    @pl.when(col < active_last)
                    def _():
                        i_put_p[it, c_p] = i_got_p[it, c_p] + i_own[it, c_p]
                        i_up(it, c_p, i_put_p.at[it, c_p]).start()

                @pl.when(jnp.logical_and(jnp.logical_and(c_s >= 0, c_s < n_in), col < active_last))
                def _():
                    i_down(it, c_s, i_own.at[it, c_s]).wait_recv()

                    @pl.when(col > 0)
                    def _():
                        i_put_s[it, c_s] = i_got_s[it, c_s] + i_own[it, c_s]
                        i_down(it, c_s, i_put_s.at[it, c_s]).start()
                return carry

            lax.fori_loop(0, n_in + lag_max, step, 0)
            for c in range(n_in):
                before = jnp.where(is_first, 0.0, i_got_p[it, c])
                after = jnp.where(col == active_last, 0.0, i_got_s[it, c])
                inner[c * wide_i:(c + 1) * wide_i, :] = before + i_own[it, c] + after
            acc[...] = product(stacked(inner[...]), r_hi[...], r_lo[...], NT)

        @pl.when(col > active_last)
        def _():
            acc[...] = jnp.zeros_like(acc)

    def drain_solve(it):
        for c in range(n_in):
            @pl.when(col < active_last)
            def _():
                i_up(it, c, i_own.at[it, c]).wait_send()

            @pl.when(jnp.logical_and(col > 0, col <= active_last))
            def _():
                i_down(it, c, i_own.at[it, c]).wait_send()

    def f_up(q, src):
        b = n_col - 1 - q // n_half
        return line(src, f_got_p.at[b, lax.rem(q, n_half)], f_sem, 0, q, 1)

    def f_down(q, src):
        b = q // n_half
        return line(src, f_got_s.at[b, lax.rem(q, n_half)], f_sem, 1, q, -1)

    def finish():
        f_cat = stacked(field[...])
        per = width // rows_c
        for c in range(chunks):
            value = fit(c, f_cat)
            for b in range(n_col):
                f_own[b, c // per, :, (c % per) * rows_c:(c % per + 1) * rows_c] = value[b * blk:(b + 1) * blk, :]
        total_q = n_col * n_half

        @pl.when(is_first)
        def _():
            def send(q, carry):
                f_up(q, f_own.at[n_col - 1 - q // n_half, lax.rem(q, n_half)]).start()
                return carry
            lax.fori_loop(0, total_q - n_half, send, 0)

        @pl.when(is_last)
        def _():
            def send(q, carry):
                f_down(q, f_own.at[q // n_half, lax.rem(q, n_half)]).start()
                return carry
            lax.fori_loop(0, total_q - n_half, send, 0)

        middle = jnp.logical_and(col > 0, col < n_col - 1)
        lag = jnp.where(middle, 2 * (n_col - 1 - 2 * col), 0)
        lag_s = jnp.clip(lag, 0, total_q)
        lag_p = jnp.clip(-lag, 0, total_q)
        lag_max = min(total_q, 2 * max(n_col - 3, 0))

        def step(i, carry):
            q_p = i - lag_p
            q_s = i - lag_s
            b_p = n_col - 1 - q_p // n_half
            h_p = lax.rem(q_p, n_half)
            b_s = q_s // n_half
            h_s = lax.rem(q_s, n_half)

            @pl.when(jnp.logical_and(jnp.logical_and(q_p >= 0, q_p < total_q - col * n_half), col > 0))
            def _():
                f_up(q_p, f_own.at[b_p, h_p]).wait_recv()

                @pl.when(b_p > col)
                def _():
                    f_put_p[b_p, h_p] = f_got_p[b_p, h_p] + f_own[b_p, h_p]
                    f_up(q_p, f_put_p.at[b_p, h_p]).start()

            @pl.when(jnp.logical_and(jnp.logical_and(q_s >= 0, q_s < (col + 1) * n_half), col < n_col - 1))
            def _():
                f_down(q_s, f_own.at[b_s, h_s]).wait_recv()

                @pl.when(b_s < col)
                def _():
                    f_put_s[b_s, h_s] = f_got_s[b_s, h_s] + f_own[b_s, h_s]
                    f_down(q_s, f_put_s.at[b_s, h_s]).start()
            return carry

        lax.fori_loop(0, total_q + lag_max, step, 0)
        for h in range(n_half):
            before = jnp.where(is_first, 0.0, f_got_p[col, h])
            after = jnp.where(is_last, 0.0, f_got_s[col, h])
            residual[:, h * width:(h + 1) * width] = -(before + f_own[col, h] + after)

        def drain(q, carry):
            @pl.when(q < (n_col - 1 - col) * n_half)
            def _():
                f_up(q, f_own.at[0, 0]).wait_send()

            @pl.when(q < col * n_half)
            def _():
                f_down(q, f_own.at[0, 0]).wait_send()
            return carry

        lax.fori_loop(0, total_q, drain, 0)

    for it in range(ITERS):
        fit_and_sum(it)
        row_sum(2 * it)
        solve(it)
        row_sum(2 * it + 1)
        field[...] = field[...] - acc[...]
        if it == 0:
            correction[...] = -acc[...]
        else:
            correction[...] = correction[...] - acc[...]
    finish()
    for it in range(ITERS):
        drain_sum(it)
        drain_solve(it)


def local(n_row, n_col, dosage, phenotypes, solution, inverse_factor):
    rows, cols = dosage.shape
    blk = phenotypes.shape[1]
    n_p = solution.shape[1]
    n_rb = inverse_factor.shape[1]
    chunks = 8
    rows_c = rows // chunks
    n_in = 4
    n_half = 2
    n_x = n_row // 2
    big = pltpu.VMEM((ITERS, chunks, n_p, rows_c), F32)
    last = pltpu.VMEM((n_col, n_half, blk, rows // n_half), F32)
    mid = pltpu.VMEM((ITERS, n_in, n_p // n_in, n_rb), F32)
    k = 2 * ITERS
    scratch = [
        pltpu.VMEM((chunks, rows_c, cols), F32),
        pltpu.VMEM((chunks, rows_c, cols), BF16),
        pltpu.VMEM((chunks, rows_c, cols), BF16),
        pltpu.VMEM((blk, rows), F32),
        pltpu.VMEM((chunks, n_p, rows_c), F32),
        pltpu.VMEM((n_p, cols), F32),
        pltpu.VMEM((n_p, cols), F32),
        pltpu.VMEM(inverse_factor.shape, F32),
        pltpu.VMEM(inverse_factor.shape, BF16),
        pltpu.VMEM(inverse_factor.shape, BF16),
        big, big, big, big, big,
        last, last, last, last, last,
        pltpu.VMEM((n_p, cols), F32),
        pltpu.VMEM((k, n_p // 2, cols), F32),
        pltpu.VMEM((k, n_p // 2, cols), F32),
        pltpu.VMEM((k, max(n_x - 1, 1), n_p // 2, cols), F32),
        pltpu.VMEM((k, 2, n_p // 2, cols), F32),
        pltpu.VMEM((k, 3, n_p // 2, cols), F32),
        mid, mid, mid, mid, mid,
        pltpu.VMEM((n_p, n_rb), F32),
        pltpu.SemaphoreType.DMA((3,)),
        pltpu.SemaphoreType.DMA((chunks,)),
        pltpu.SemaphoreType.DMA((ITERS, 2, 2, chunks)),
        pltpu.SemaphoreType.DMA((2, 2, n_col * n_half)),
        pltpu.SemaphoreType.DMA((k, 4)),
        pltpu.SemaphoreType.DMA((k, max(n_x - 1, 1))),
        pltpu.SemaphoreType.DMA((k, max(n_x - 1, 1))),
        pltpu.SemaphoreType.DMA((ITERS, 2, 2, n_in)),
    ]
    any_spec = pl.BlockSpec(memory_space=pl.ANY)
    vmem_spec = pl.BlockSpec(memory_space=pltpu.VMEM)
    residual, correction = pl.pallas_call(
        functools.partial(kernel, (n_row, n_col, chunks, n_in)),
        out_shape=(
            jax.ShapeDtypeStruct((blk, rows), F32),
            jax.ShapeDtypeStruct((n_p, cols), F32),
        ),
        in_specs=[any_spec] * 4,
        out_specs=(vmem_spec, vmem_spec),
        scratch_shapes=scratch,
        compiler_params=pltpu.CompilerParams(collective_id=0, has_side_effects=True),
    )(dosage, phenotypes.T, solution.T, inverse_factor)
    return residual.T, correction.T


def solution(mesh):
    return jax.shard_map(
        functools.partial(local, mesh.shape["row"], mesh.shape["col"]),
        mesh=mesh,
        in_specs=(
            P(("grp", "row"), "col"),
            P(("grp", "row"), "col"),
            P(("grp", "col"), None),
            P(("grp", "col"), "row"),
        ),
        out_specs=(P(("grp", "row"), "col"), P(("grp", "col"), None)),
        check_vma=False,
    )
```

time: 355 us -> 107 us (0.30)
  waiting for transfers between devices: 262 us -> 0 us
  Pallas kernels: 0 us -> 103 us
  matrix products: 42.4 us -> 0 us
  blocking collectives: 31.1 us -> 0 us
  between operations: 13.9 us -> 0.64 us
  other arithmetic: 5.01 us -> 0 us
    psum x6 -> x0, waiting for transfers between devices: 194 us -> none  [the longest x2 70.4 us: local(): lax.psum(transposed_product(inverse_factor, lax.psum(partial_value, 'row'...]
    pallas_call x0 -> x1, Pallas kernels: none -> 103 us  [local(): pl.pallas_call(functools.partial(kernel, (n_row, n_col, chunks, n_in)), o...]
    reduce_scatter x3 -> x0, waiting for transfers between devices: 67.9 us -> none  [residual_parts(): lax.psum_scatter(fitted, 'col', scatter_dimension=1, tiled=True)]
    dot_general x9 -> x0, matrix products: 42.4 us -> none  [the longest x5 26.7 us: plain_product(): jnp.dot(left, right, precision=lax.Precision.HIGHEST, preferred_element_t...]
    all_gather x2 -> x0, blocking collectives: 31.1 us -> none  [local(): lax.all_gather(own, 'col', axis=1, tiled=True)]
  transfers between devices with their start and end apart: 9 -> 0, of which waited for: 9 -> 0; matrix products, arithmetic and copies ran while one was open for 0% -> 0% of each run, Pallas kernels for 0% -> 0%
where the time goes in v1:
time: 107 us
  Pallas kernels  103 us (96%)
  local copies, waits for them, and re-layouts  3.14 us (3%)
    pallas_call x1, Pallas kernels, local(): pl.pallas_call(functools.partial(kernel, (n_row, n_col, chunks, n_in)), o...  103 us
    unnamed x2, local copies, waits for them, and re-layouts  3.14 us

profile of v1, /device:TPU:0, one launch (start us, length us, event | category | flops | bytes accessed | tf_op | source)
XLA Modules:
  0.0 107.2 jit_solution(17811167269713155784)
XLA Ops:
  0.6 103.5 %shard_map.59 = (f32[16,2048]{1,0:T(8,128)}, f32[64,512]{1,0:T(8,128)}) custom-call(f32[2048,512]{1,0:T(8,128)} %dosage.1, f32[16,2048]{1,0:T(8,128)} %bitcast.4, f32[64,512]{1,0:T(8,128)} %bitcast.5, f32[512,512]{1,0:T(8,128)} %factor.1), custom_call_target="tpu_custom_call" | custom-call | tf_op jit(solution)/shard_map/pallas_call | solution.py:460
  104.1 1.6 %copy.8 = f32[2048,16]{0,1:T(8,128)} copy(f32[2048,16]{0,1:T(8,128)} %bitcast.7) | data formatting | bytes 262144
  105.7 1.6 %copy.9 = f32[512,64]{0,1:T(8,128)} copy(f32[512,64]{0,1:T(8,128)} %bitcast.6) | data formatting | bytes 262144

commit v2 on v1

v2 whole, which is shorter than its diff:
```python
import functools

import jax
import jax.numpy as jnp
from jax import lax
from jax.experimental import pallas as pl
from jax.experimental.pallas import tpu as pltpu
from jax.sharding import PartitionSpec as P

ITERS = 2
MESH = pl.DeviceIdType.MESH
F32 = jnp.float32
BF16 = jnp.bfloat16
COST_FIT = 0.25
COST_STEP = 0.3
PITCH = 0.5
NN = (((1,), (0,)), ((), ()))
NT = (((1,), (1,)), ((), ()))


def split(value):
    high = value.astype(BF16)
    low = (value - high.astype(F32)).astype(BF16)
    return high, low


def product(left, right_high, right_low, dims):
    count = left.shape[0] // 2
    main = lax.dot_general(left, right_high, dims, preferred_element_type=F32)
    rest = lax.dot_general(left[:count], right_low, dims, preferred_element_type=F32)
    return main[:count] + (main[count:] + rest)


def stacked(value):
    return jnp.concatenate(split(value), axis=0)


def kernel(cfg, dosage, pheno, start, factor, residual, correction, *scratch):
    (n_row, n_col, streams, chunks, n_in, lag, lag_in, lag_f) = cfg
    (d_f32, d_hi, d_lo, y_in, y_pad, f_in, field, total_change, r_f32, r_hi, r_lo,
     own, got_p, got_s, put_p, put_s,
     f_own, f_got_p, f_got_s, f_put_p, f_put_s,
     acc, pair_got, cross_put, cross_got, back_put, back_got,
     i_own, i_got_p, i_got_s, i_put_p, i_put_s,
     load_sem, d_sem, a_sem, f_sem, pair_sem, cross_ssem, cross_rsem, i_sem) = scratch
    rows_c = d_hi.shape[1]
    n_p = field.shape[1]
    half = n_p // 2
    blk = pheno.shape[0]
    sub = blk // streams
    n_half = f_own.shape[2]
    width = f_own.shape[4]
    n_x = n_row // 2

    row = lax.axis_index("row")
    col = lax.axis_index("col")
    core = lax.rem(row, 2)
    x = row // 2
    partner = {"row": row + 1 - 2 * core}
    is_first = col == 0
    is_last = col == n_col - 1

    loads = []
    for k, (src, dst) in enumerate(((start, f_in), (pheno, y_in), (factor, r_f32))):
        loads.append(pltpu.make_async_copy(src, dst, load_sem.at[k]))

    def d_copy(c):
        return pltpu.make_async_copy(
            dosage.at[pl.ds(c * rows_c, rows_c), :], d_f32.at[c], d_sem.at[c])

    barrier = pltpu.get_barrier_semaphore()

    @pl.when(col > 0)
    def _():
        pl.semaphore_signal(barrier, inc=1, device_id={"col": col - 1}, device_id_type=MESH)

    @pl.when(col < n_col - 1)
    def _():
        pl.semaphore_signal(barrier, inc=1, device_id={"col": col + 1}, device_id_type=MESH)

    pl.semaphore_signal(barrier, inc=1, device_id=partner, device_id_type=MESH)
    for d in range(1, n_x):
        other = lax.rem(x + d, n_x) * 2 + core
        pl.semaphore_signal(barrier, inc=1, device_id={"row": other}, device_id_type=MESH)

    loads[0].start()
    loads[1].start()
    for c in range(chunks):
        d_copy(c).start()
    loads[2].start()

    def enter():
        up_down = jnp.where(is_first, 0, 1) + jnp.where(is_last, 0, 1)
        pl.semaphore_wait(barrier, n_x + up_down)

    loads[0].wait()
    for s in range(streams):
        for b in range(n_col):
            at = b * blk + s * sub
            field[s, b * sub:(b + 1) * sub, :] = f_in[at:at + sub, :]
    loads[1].wait()
    for s in range(streams):
        for c in range(chunks):
            y_c = y_in[s * sub:(s + 1) * sub, c * rows_c:(c + 1) * rows_c]
            for b in range(n_col):
                y_pad[s, c, b * sub:(b + 1) * sub, :] = jnp.where(col == b, y_c, 0.0)

    def line(src, dst, sems, way, c, step):
        return pltpu.make_async_remote_copy(
            src_ref=src, dst_ref=dst, send_sem=sems.at[way, 0, c], recv_sem=sems.at[way, 1, c],
            device_id={"col": jnp.clip(col + step, 0, n_col - 1)}, device_id_type=MESH)

    def within(value, low, high):
        return jnp.logical_and(value >= low, value < high)

    done = set()

    def fit(s, c, f_cat):
        if c not in done:
            done.add(c)
            d_copy(c).wait()
            high, low = split(d_f32[c])
            d_hi[c] = high
            d_lo[c] = low
        return product(f_cat, d_hi[c], d_lo[c], NT) - y_pad[s, c]

    def up(s, it, c, src):
        return line(src, got_p.at[it, s, c], a_sem.at[it, s], 0, c, 1)

    def down(s, it, c, src):
        return line(src, got_s.at[it, s, c], a_sem.at[it, s], 1, c, -1)

    def fit_and_sum(s, it):
        f_cat = stacked(field[s])
        for c in range(chunks):
            own[it, s, c] = fit(s, c, f_cat)
            if "enter" not in done:
                done.add("enter")
                enter()

            @pl.when(is_first)
            def _():
                up(s, it, c, own.at[it, s, c]).start()

            @pl.when(is_last)
            def _():
                down(s, it, c, own.at[it, s, c]).start()
            yield COST_FIT, (0.0 if c < chunks - 1 else 2.4 - chunks * COST_FIT)
        acc[s] = jnp.zeros_like(acc[s])
        lag_p = lag * (col - 1)
        lag_s = lag * (n_col - 2 - col)
        steps = chunks + lag * (n_col - 2)
        for i in range(steps):
            c_p = i - lag_p
            c_s = i - lag_s

            @pl.when(jnp.logical_and(within(c_p, 0, chunks), col > 0))
            def _():
                up(s, it, c_p, own.at[it, s, c_p]).wait_recv()

                @pl.when(col < n_col - 1)
                def _():
                    put_p[it, s, c_p] = got_p[it, s, c_p] + own[it, s, c_p]
                    up(s, it, c_p, put_p.at[it, s, c_p]).start()

            @pl.when(jnp.logical_and(within(c_s, 0, chunks), col < n_col - 1))
            def _():
                down(s, it, c_s, own.at[it, s, c_s]).wait_recv()

                @pl.when(col > 0)
                def _():
                    put_s[it, s, c_s] = got_s[it, s, c_s] + own[it, s, c_s]
                    down(s, it, c_s, put_s.at[it, s, c_s]).start()

            c = jnp.minimum(jnp.where(is_first, chunks + steps, c_p), jnp.where(is_last, chunks + steps, c_s))

            @pl.when(within(c, 0, chunks))
            def _():
                before = jnp.where(is_first, 0.0, got_p[it, s, c])
                after = jnp.where(is_last, 0.0, got_s[it, s, c])
                resid = before + own[it, s, c] + after
                acc[s] += product(stacked(resid), d_hi[c], d_lo[c], NN)
            yield COST_STEP, PITCH

    def drain_sum(s, it):
        def step(c, carry):
            @pl.when(col < n_col - 1)
            def _():
                up(s, it, c, own.at[it, s, c]).wait_send()

            @pl.when(col > 0)
            def _():
                down(s, it, c, own.at[it, s, c]).wait_send()
            return carry

        lax.fori_loop(0, chunks, step, 0)

    sent = []

    def row_sum(s, k):
        for h in range(2):
            back_put[k, s, h] = acc[s, h * half:(h + 1) * half, :]
        first = pltpu.make_async_remote_copy(
            src_ref=back_put.at[k, s, 1 - core], dst_ref=pair_got.at[k, s],
            send_sem=pair_sem.at[k, s, 0], recv_sem=pair_sem.at[k, s, 1],
            device_id=partner, device_id_type=MESH)
        first.start()
        yield 0.2, 1.0
        first.wait_recv()
        cross_put[k, s] = back_put[k, s, core] + pair_got[k, s]
        sends = []
        for d in range(1, n_x):
            other = lax.rem(x + d, n_x) * 2 + core
            sends.append(pltpu.make_async_remote_copy(
                src_ref=cross_put.at[k, s], dst_ref=cross_got.at[k, s, d - 1],
                send_sem=cross_ssem.at[k, s, d - 1], recv_sem=cross_rsem.at[k, s, d - 1],
                device_id={"row": other}, device_id_type=MESH))
            sends[-1].start()
        yield 0.1, 2.4
        parts = [cross_put[k, s]]
        for d in range(1, n_x):
            sends[d - 1].wait_recv()
            parts.append(cross_got[k, s, d - 1])
        total = None
        for chip in range(n_x):
            here = parts[0]
            for d in range(1, n_x):
                here = jnp.where(lax.rem(x - d + n_x, n_x) == chip, parts[d], here)
            total = here if total is None else total + here
        back_got[k, s, 2] = total
        last = pltpu.make_async_remote_copy(
            src_ref=back_got.at[k, s, 2], dst_ref=back_got.at[k, s, core],
            send_sem=pair_sem.at[k, s, 2], recv_sem=pair_sem.at[k, s, 3],
            device_id=partner, device_id_type=MESH)
        last.start()
        yield 0.1, 1.0
        last.wait_recv()
        theirs = back_got[k, s, 1 - core]
        mine = back_got[k, s, 2]
        acc[s, 0:half, :] = jnp.where(core == 0, mine, theirs)
        acc[s, half:, :] = jnp.where(core == 0, theirs, mine)
        sent.extend((first, last, *sends))

    n_rb = r_hi.shape[1]
    n_cb = r_hi.shape[0]
    active_last = jnp.minimum(((row + 1) * n_rb + n_cb - 1) // n_cb - 1, n_col - 1)
    wide_i = n_p // n_in

    def i_up(s, it, c, src):
        return line(src, i_got_p.at[it, s, c], i_sem.at[it, s], 0, c, 1)

    def i_down(s, it, c, src):
        return line(src, i_got_s.at[it, s, c], i_sem.at[it, s], 1, c, -1)

    def solve(s, it):
        if "factor" not in done:
            done.add("factor")
            loads[2].wait()
            high, low = split(r_f32[...])
            r_hi[...] = high
            r_lo[...] = low

        @pl.when(col <= active_last)
        def _():
            part = product(stacked(acc[s]), r_hi[...], r_lo[...], NN)
            for c in range(n_in):
                i_own[it, s, c] = part[c * wide_i:(c + 1) * wide_i]

            @pl.when(jnp.logical_and(is_first, active_last > 0))
            def _():
                for c in range(n_in):
                    i_up(s, it, c, i_own.at[it, s, c]).start()

            @pl.when(jnp.logical_and(col == active_last, active_last > 0))
            def _():
                for c in range(n_in):
                    i_down(s, it, c, i_own.at[it, s, c]).start()
        yield 0.4, 2.2
        lag_p = lag_in * (col - 1)
        lag_s = lag_in * (active_last - col - 1)
        steps = n_in + lag_in * (n_col - 2)
        for i in range(steps):
            c_p = i - lag_p
            c_s = i - lag_s

            @pl.when(jnp.logical_and(within(c_p, 0, n_in), jnp.logical_and(col > 0, col <= active_last)))
            def _():
                i_up(s, it, c_p, i_own.at[it, s, c_p]).wait_recv()

                @pl.when(col < active_last)
                def _():
                    i_put_p[it, s, c_p] = i_got_p[it, s, c_p] + i_own[it, s, c_p]
                    i_up(s, it, c_p, i_put_p.at[it, s, c_p]).start()

            @pl.when(jnp.logical_and(within(c_s, 0, n_in), col < active_last))
            def _():
                i_down(s, it, c_s, i_own.at[it, s, c_s]).wait_recv()

                @pl.when(col > 0)
                def _():
                    i_put_s[it, s, c_s] = i_got_s[it, s, c_s] + i_own[it, s, c_s]
                    i_down(s, it, c_s, i_put_s.at[it, s, c_s]).start()
            if i < steps - 1:
                yield 0.05, 2.2 / lag_in

        @pl.when(col <= active_last)
        def _():
            inner = []
            for c in range(n_in):
                before = jnp.where(is_first, 0.0, i_got_p[it, s, c])
                after = jnp.where(col == active_last, 0.0, i_got_s[it, s, c])
                inner.append(before + i_own[it, s, c] + after)
            acc[s] = product(stacked(jnp.concatenate(inner, axis=0)), r_hi[...], r_lo[...], NT)

        @pl.when(col > active_last)
        def _():
            acc[s] = jnp.zeros_like(acc[s])

    def drain_solve(s, it):
        for c in range(n_in):
            @pl.when(col < active_last)
            def _():
                i_up(s, it, c, i_own.at[it, s, c]).wait_send()

            @pl.when(jnp.logical_and(col > 0, col <= active_last))
            def _():
                i_down(s, it, c, i_own.at[it, s, c]).wait_send()

    total_q = n_col * n_half

    def f_up(s, q, src):
        b = n_col - 1 - q // n_half
        return line(src, f_got_p.at[s, b, lax.rem(q, n_half)], f_sem.at[s], 0, q, 1)

    def f_down(s, q, src):
        b = q // n_half
        return line(src, f_got_s.at[s, b, lax.rem(q, n_half)], f_sem.at[s], 1, q, -1)

    def finish(s):
        f_cat = stacked(field[s])
        per = width // rows_c
        for c in range(chunks):
            value = fit(s, c, f_cat)
            for b in range(n_col):
                f_own[s, b, c // per, :, (c % per) * rows_c:(c % per + 1) * rows_c] = value[b * sub:(b + 1) * sub, :]
            if c < chunks - 1:
                yield COST_FIT, 0.0

        @pl.when(is_first)
        def _():
            for q in range(total_q - n_half):
                f_up(s, q, f_own.at[s, n_col - 1 - q // n_half, q % n_half]).start()

        @pl.when(is_last)
        def _():
            for q in range(total_q - n_half):
                f_down(s, q, f_own.at[s, q // n_half, q % n_half]).start()
        yield COST_FIT, 2.4
        lag_p = lag_f * (col - 1)
        lag_s = lag_f * (n_col - 2 - col)
        steps = max(total_q - z * n_half + lag_f * (z - 1) for z in range(1, n_col))
        for i in range(steps):
            q_p = i - lag_p
            q_s = i - lag_s
            b_p = n_col - 1 - q_p // n_half
            b_s = q_s // n_half

            @pl.when(jnp.logical_and(within(q_p, 0, total_q - col * n_half), col > 0))
            def _():
                h_p = lax.rem(q_p, n_half)
                f_up(s, q_p, f_own.at[s, b_p, h_p]).wait_recv()

                @pl.when(b_p > col)
                def _():
                    f_put_p[s, b_p, h_p] = f_got_p[s, b_p, h_p] + f_own[s, b_p, h_p]
                    f_up(s, q_p, f_put_p.at[s, b_p, h_p]).start()

            @pl.when(jnp.logical_and(within(q_s, 0, (col + 1) * n_half), col < n_col - 1))
            def _():
                h_s = lax.rem(q_s, n_half)
                f_down(s, q_s, f_own.at[s, b_s, h_s]).wait_recv()

                @pl.when(b_s < col)
                def _():
                    f_put_s[s, b_s, h_s] = f_got_s[s, b_s, h_s] + f_own[s, b_s, h_s]
                    f_down(s, q_s, f_put_s.at[s, b_s, h_s]).start()
            yield 0.1, PITCH
        for h in range(n_half):
            before = jnp.where(is_first, 0.0, f_got_p[s, col, h])
            after = jnp.where(is_last, 0.0, f_got_s[s, col, h])
            residual[s * sub:(s + 1) * sub, h * width:(h + 1) * width] = -(before + f_own[s, col, h] + after)

    def drain_finish(s):
        def drain(q, carry):
            @pl.when(q < (n_col - 1 - col) * n_half)
            def _():
                f_up(s, q, f_own.at[s, 0, 0]).wait_send()

            @pl.when(q < col * n_half)
            def _():
                f_down(s, q, f_own.at[s, 0, 0]).wait_send()
            return carry

        lax.fori_loop(0, total_q, drain, 0)

    def stream(s):
        for it in range(ITERS):
            yield from fit_and_sum(s, it)
            yield from row_sum(s, 2 * it)
            yield from solve(s, it)
            yield from row_sum(s, 2 * it + 1)
            change = acc[s]
            field[s] = field[s] - change
            if it == 0:
                total_change[s] = -change
            else:
                for b in range(n_col):
                    at = b * blk + s * sub
                    correction[at:at + sub, :] = total_change[s, b * sub:(b + 1) * sub, :] - change[b * sub:(b + 1) * sub]
        yield from finish(s)

    work = [[0.001 * s, s, stream(s)] for s in range(streams)]
    now = 0.0
    while work:
        work.sort(key=lambda entry: entry[:2])
        entry = work[0]
        now = max(now, entry[0])
        step = next(entry[2], None)
        if step is None:
            work.remove(entry)
            continue
        now += step[0]
        entry[0] = now + step[1]

    for copy in sent:
        copy.wait_send()
    for s in range(streams):
        for it in range(ITERS):
            drain_sum(s, it)
            drain_solve(s, it)
        drain_finish(s)


def local(n_row, n_col, dosage, phenotypes, solution, inverse_factor):
    rows, cols = dosage.shape
    blk = phenotypes.shape[1]
    n_rb = inverse_factor.shape[1]
    streams = 2
    n_all = solution.shape[1]
    n_p = n_all // streams
    chunks = 8
    rows_c = rows // chunks
    n_in = 2
    n_half = 2
    n_x = n_row // 2
    lags = (3, 2, 3) if n_col <= 4 else (1, 1, 1)
    big = pltpu.VMEM((ITERS, streams, chunks, n_p, rows_c), F32)
    last = pltpu.VMEM((streams, n_col, n_half, blk // streams, rows // n_half), F32)
    mid = pltpu.VMEM((ITERS, streams, n_in, n_p // n_in, n_rb), F32)
    vec = pltpu.VMEM((streams, n_p, cols), F32)
    k = 2 * ITERS
    scratch = [
        pltpu.VMEM((chunks, rows_c, cols), F32),
        pltpu.VMEM((chunks, rows_c, cols), BF16),
        pltpu.VMEM((chunks, rows_c, cols), BF16),
        pltpu.VMEM((blk, rows), F32),
        pltpu.VMEM((streams, chunks, n_p, rows_c), F32),
        pltpu.VMEM((n_all, cols), F32),
        vec, vec,
        pltpu.VMEM(inverse_factor.shape, F32),
        pltpu.VMEM(inverse_factor.shape, BF16),
        pltpu.VMEM(inverse_factor.shape, BF16),
        big, big, big, big, big,
        last, last, last, last, last,
        vec,
        pltpu.VMEM((k, streams, n_p // 2, cols), F32),
        pltpu.VMEM((k, streams, n_p // 2, cols), F32),
        pltpu.VMEM((k, streams, max(n_x - 1, 1), n_p // 2, cols), F32),
        pltpu.VMEM((k, streams, 2, n_p // 2, cols), F32),
        pltpu.VMEM((k, streams, 3, n_p // 2, cols), F32),
        mid, mid, mid, mid, mid,
        pltpu.SemaphoreType.DMA((3,)),
        pltpu.SemaphoreType.DMA((chunks,)),
        pltpu.SemaphoreType.DMA((ITERS, streams, 2, 2, chunks)),
        pltpu.SemaphoreType.DMA((streams, 2, 2, n_col * n_half)),
        pltpu.SemaphoreType.DMA((k, streams, 4)),
        pltpu.SemaphoreType.DMA((k, streams, max(n_x - 1, 1))),
        pltpu.SemaphoreType.DMA((k, streams, max(n_x - 1, 1))),
        pltpu.SemaphoreType.DMA((ITERS, streams, 2, 2, n_in)),
    ]
    any_spec = pl.BlockSpec(memory_space=pl.ANY)
    vmem_spec = pl.BlockSpec(memory_space=pltpu.VMEM)
    residual, correction = pl.pallas_call(
        functools.partial(kernel, (n_row, n_col, streams, chunks, n_in, *lags)),
        out_shape=(
            jax.ShapeDtypeStruct((blk, rows), F32),
            jax.ShapeDtypeStruct((n_all, cols), F32),
        ),
        in_specs=[any_spec] * 4,
        out_specs=(vmem_spec, vmem_spec),
        scratch_shapes=scratch,
        compiler_params=pltpu.CompilerParams(collective_id=0, has_side_effects=True),
    )(dosage, phenotypes.T, solution.T, inverse_factor)
    return residual.T, correction.T


def solution(mesh):
    return jax.shard_map(
        functools.partial(local, mesh.shape["row"], mesh.shape["col"]),
        mesh=mesh,
        in_specs=(
            P(("grp", "row"), "col"),
            P(("grp", "row"), "col"),
            P(("grp", "col"), None),
            P(("grp", "col"), "row"),
        ),
        out_specs=(P(("grp", "row"), "col"), P(("grp", "col"), None)),
        check_vma=False,
    )
```

time: 107 us -> 109 us (1.019)
  Pallas kernels: 103 us -> 105 us
    pallas_call x1, Pallas kernels: 103 us -> 105 us  [local(): pl.pallas_call(functools.partial(kernel, (n_row, n_col, streams, chunks,...]
where the time goes in v2:
time: 109 us
  Pallas kernels  105 us (96%)
  local copies, waits for them, and re-layouts  3.14 us (3%)
    pallas_call x1, Pallas kernels, local(): pl.pallas_call(functools.partial(kernel, (n_row, n_col, streams, chunks,...  105 us
    unnamed x2, local copies, waits for them, and re-layouts  3.14 us

profile of v2, /device:TPU:0, one launch (start us, length us, event | category | flops | bytes accessed | tf_op | source)
XLA Modules:
  0.0 109.2 jit_solution(947606015937551036)
XLA Ops:
  0.6 105.4 %shard_map.59 = (f32[16,2048]{1,0:T(8,128)}, f32[64,512]{1,0:T(8,128)}) custom-call(f32[2048,512]{1,0:T(8,128)} %dosage.1, f32[16,2048]{1,0:T(8,128)} %bitcast.4, f32[64,512]{1,0:T(8,128)} %bitcast.5, f32[512,512]{1,0:T(8,128)} %factor.1), custom_call_target="tpu_custom_call" | custom-call | tf_op jit(solution)/shard_map/pallas_call | solution.py:493
  106.0 1.6 %copy.8 = f32[2048,16]{0,1:T(8,128)} copy(f32[2048,16]{0,1:T(8,128)} %bitcast.7) | data formatting | bytes 262144
  107.6 1.6 %copy.9 = f32[512,64]{0,1:T(8,128)} copy(f32[512,64]{0,1:T(8,128)} %bitcast.6) | data formatting | bytes 262144

commit v3 on v1

--- a/solution.py
+++ b/solution.py
@@ -133,10 +133,10 @@
         lax.fori_loop(0, chunks, make, 0)
         acc[...] = jnp.zeros_like(acc)
         middle = jnp.logical_and(col > 0, col < n_col - 1)
-        lag = jnp.where(middle, 2 * (n_col - 1 - 2 * col), 0)
+        lag = jnp.where(middle, 4 * (n_col - 1 - 2 * col), 0)
         lag_s = jnp.clip(lag, 0, chunks)
         lag_p = jnp.clip(-lag, 0, chunks)
-        lag_max = min(chunks, 2 * max(n_col - 3, 0))
+        lag_max = min(chunks, 4 * max(n_col - 3, 0))
 
         def step(i, carry):
             c_p = i - lag_p
@@ -345,10 +345,10 @@
             lax.fori_loop(0, total_q - n_half, send, 0)
 
         middle = jnp.logical_and(col > 0, col < n_col - 1)
-        lag = jnp.where(middle, 2 * (n_col - 1 - 2 * col), 0)
+        lag = jnp.where(middle, 4 * (n_col - 1 - 2 * col), 0)
         lag_s = jnp.clip(lag, 0, total_q)
         lag_p = jnp.clip(-lag, 0, total_q)
-        lag_max = min(total_q, 2 * max(n_col - 3, 0))
+        lag_max = min(total_q, 4 * max(n_col - 3, 0))
 
         def step(i, carry):
             q_p = i - lag_p
@@ -416,10 +416,10 @@
     blk = phenotypes.shape[1]
     n_p = solution.shape[1]
     n_rb = inverse_factor.shape[1]
-    chunks = 8
+    chunks = 16
     rows_c = rows // chunks
     n_in = 4
-    n_half = 2
+    n_half = 4
     n_x = n_row // 2
     big = pltpu.VMEM((ITERS, chunks, n_p, rows_c), F32)
     last = pltpu.VMEM((n_col, n_half, blk, rows // n_half), F32)

time: 107 us -> 105 us (0.981)
  Pallas kernels: 103 us -> 101 us
    pallas_call x1, Pallas kernels: 103 us -> 101 us  [local(): pl.pallas_call(functools.partial(kernel, (n_row, n_col, chunks, n_in)), o...]
where the time goes in v3:
time: 105 us
  Pallas kernels  101 us (96%)
  local copies, waits for them, and re-layouts  3.14 us (3%)
    pallas_call x1, Pallas kernels, local(): pl.pallas_call(functools.partial(kernel, (n_row, n_col, chunks, n_in)), o...  101 us
    unnamed x2, local copies, waits for them, and re-layouts  3.14 us

profile of v3, /device:TPU:0, one launch (start us, length us, event | category | flops | bytes accessed | tf_op | source)
XLA Modules:
  0.0 104.6 jit_solution(2973216575205469285)
XLA Ops:
  0.6 100.9 %shard_map.59 = (f32[16,2048]{1,0:T(8,128)}, f32[64,512]{1,0:T(8,128)}) custom-call(f32[2048,512]{1,0:T(8,128)} %dosage.1, f32[16,2048]{1,0:T(8,128)} %bitcast.4, f32[64,512]{1,0:T(8,128)} %bitcast.5, f32[512,512]{1,0:T(8,128)} %factor.1), custom_call_target="tpu_custom_call" | custom-call | tf_op jit(solution)/shard_map/pallas_call | solution.py:460
  101.5 1.6 %copy.8 = f32[2048,16]{0,1:T(8,128)} copy(f32[2048,16]{0,1:T(8,128)} %bitcast.7) | data formatting | bytes 262144
  103.1 1.6 %copy.9 = f32[512,64]{0,1:T(8,128)} copy(f32[512,64]{0,1:T(8,128)} %bitcast.6) | data formatting | bytes 262144
